TPU v7x, 256 devices: a whole 4x4x8 slice. The times are simulated.
256 devices in a mesh: row: 8 (over x, z_hi), col: 8 (over z_lo, core), layer: 4 (over y).
Axes of the slice: x: 4, y: 4, z: 8 (z_hi: 2, z_lo: 4; z = z_hi * 4 + z_lo), core: 2. Of those that a mesh axis runs over, the one named last changes fastest.
Arguments:
- amplitudes: float32 [4096, 2048], P('row', ('col', 'layer')), may hold values from -6 to 6
- integrals: float32 [2048, 16384], P(('row', 'layer'), 'col'), may hold values from -0.125 to 0.125
Outputs:
- ladder: float32 [4096, 16384], P('row', ('col', 'layer'))
All inputs are finite; a program needn't handle non-finite values.
Results may differ from a plain program's by a relative error of at most 0.000082.
Values sent between devices are 32-bit elements; how exact they have to be, the bound alone decides.
A program may use at most 64 MiB of HBM per device.

v0:
```python
import jax
import jax.numpy as jnp
from jax import lax
from jax.sharding import PartitionSpec as P


def from_root(block, axis, holder):
    block = jnp.where(lax.axis_index(axis) == holder, block, jnp.zeros_like(block))
    return lax.psum(block, axis)


def summa(amp_panel, int_panel, step_count, first_step):
    spread = lax.axis_size("col") // lax.axis_size("row")
    partial_sum = jnp.zeros((amp_panel.shape[0], int_panel.shape[1]), jnp.float32)

    def one_turn(turn_at, total):
        block_at = first_step + turn_at
        amp_block = from_root(amp_panel, "col", block_at)
        int_block = from_root(int_panel, "row", block_at // spread)
        return total + jnp.dot(
            amp_block,
            int_block,
            precision=lax.Precision.HIGHEST,
            preferred_element_type=jnp.float32,
        )

    return lax.fori_loop(0, step_count, one_turn, partial_sum)


def contract(amp_panel, int_panel, step_count, first_step):
    return summa(amp_panel, int_panel, step_count, first_step)


def shards(amplitudes, integrals):
    cols_n = lax.axis_size("col")
    layers_n = lax.axis_size("layer")
    layer_at = lax.axis_index("layer")
    amp_panel = lax.all_gather(amplitudes, "layer", axis=1, tiled=True)
    int_panel = lax.all_gather(integrals, "layer", axis=0, tiled=True)
    step_count = cols_n // layers_n
    partial_sum = contract(amp_panel, int_panel, step_count, layer_at * step_count)
    product = lax.psum_scatter(partial_sum, "layer", scatter_dimension=1, tiled=True)
    return 0.5 * product


def solution(mesh):
    in_specs = (P("row", ("col", "layer")), P(("row", "layer"), "col"))
    out_specs = P("row", ("col", "layer"))
    return jax.shard_map(shards, mesh=mesh, in_specs=in_specs, out_specs=out_specs, check_vma=False)
```

profile of v0, /device:TPU:1, one launch (start us, length us, event | category | flops | bytes accessed | tf_op | source)
XLA Modules:
  0.0 660.9 jit_solution(806559248901591180)
XLA Ops:
  6.5 0.0 all-gather.2.cloned.1.call-start
  6.5 0.7 all-gather.2.cloned.1.call-update
  7.3 12.8 %all_gather.6 = f32[512,256]{0,1:T(8,128)S(1)} all-gather(f32[512,64]{0,1:T(8,128)} %param.4), channel_id=1, replica_groups=mesh['row'=8,'col'=8,'layer'=4] {'layer'}, dimensions={1}, use_global_device_ids=true | all-gather | bytes 655360 | tf_op jit(solution)/shard_map/all_gather | solution.py:38
  20.1 0.2 copy.4
  20.3 25.9 %all-gather.2.cloned.1.call-done = f32[256,2048]{1,0:T(8,128)} async-done(((f32[64,2048]{1,0:T(8,128)}), f32[256,2048]{1,0:T(8,128)}) %all-gather.2.cloned.1.call-update) | async-done | bytes 2097168 | tf_op jit(solution)/shard_map/all_gather | solution.py:39
  46.1 555.9 %while.16 = (s32[]{:T(128)}, f32[512,2048]{1,0:T(8,128)}, s32[]{:T(128)}, f32[512,256]{1,0:T(8,128)S(1)}, f32[256,2048]{1,0:T(8,128)}, /*index=5*/s32[]{:T(128)}, u32[]{:T(128)}, u32[]{:T(128)}, u32[]{:T(128)}, s32[]{:T(128)}) while((s32[]{:T(128)}, f32[512,2048]{1,0:T(8,128)}, s32[]{:T(128)}, f32[512,256]{1,0:T(8,128)S(1)}, ...), condition=%wide.region_3.4_spmd.clone, body=%wide.region_0.3_spmd.clone.sunk | while | flops 3224633344 | bytes 31981860 | solution.py:27
  46.1 0.0 all-reduce.3.cloned.1.call-start
  46.1 0.8 broadcast_select_fusion.4
  47.0 0.0 all-reduce.3.cloned.1.call-update
  47.0 0.0 all-reduce.5.cloned.1.call-start
  47.1 3.2 broadcast_select_fusion.5
  50.2 0.0 all-reduce.5.cloned.1.call-update
  50.3 68.8 %all-reduce.3.cloned.1.call-done = f32[512,256]{1,0:T(8,128)} async-done(((f32[512,256]{1,0:T(8,128)}), f32[512,256]{1,0:T(8,128)}) %all-reduce.3.cloned.1.call-update) | async-done | bytes 524304 | tf_op jit(solution)/shard_map/while/body/eval_jaxpr/psum | solution.py:9
  119.1 198.7 %all-reduce.5.cloned.1.call-done = f32[256,2048]{1,0:T(8,128)} async-done(((f32[256,2048]{1,0:T(8,128)}), f32[256,2048]{1,0:T(8,128)}) %all-reduce.5.cloned.1.call-update) | async-done | bytes 2097168 | tf_op jit(solution)/shard_map/while/body/eval_jaxpr/psum | solution.py:9
  317.8 7.4 %select_add_fusion.2 = f32[512,2048]{1,0:T(8,128)} fusion(f32[512,2048]{1,0:T(8,128)} %get-tuple-element.215, f32[512,256]{1,0:T(8,128)} %all-reduce.3.cloned.1.call-done, f32[256,2048]{1,0:T(8,128)} %all-reduce.5.cloned.1.call-done, pred[]{:T(512)S(6)} %compare.9), kind=kOutput, calls=%fused_computation.clone.1 | convolution fusion | flops 3223322624 | bytes 11010049 | tf_op jit(solution)/shard_map/while/body/eval_jaxpr/dot_general | solution.py:20
  325.2 0.0 all-reduce.3.cloned.1.call-start
  325.2 0.8 broadcast_select_fusion.4
  326.0 0.0 all-reduce.3.cloned.1.call-update
  326.0 0.0 all-reduce.5.cloned.1.call-start
  326.1 1.6 broadcast_select_fusion.5
  327.6 0.0 all-reduce.5.cloned.1.call-update
  327.7 67.2 %all-reduce.3.cloned.1.call-done = f32[512,256]{1,0:T(8,128)} async-done(((f32[512,256]{1,0:T(8,128)}), f32[512,256]{1,0:T(8,128)}) %all-reduce.3.cloned.1.call-update) | async-done | bytes 524304 | tf_op jit(solution)/shard_map/while/body/eval_jaxpr/psum | solution.py:9
  394.8 198.5 %all-reduce.5.cloned.1.call-done = f32[256,2048]{1,0:T(8,128)} async-done(((f32[256,2048]{1,0:T(8,128)}), f32[256,2048]{1,0:T(8,128)}) %all-reduce.5.cloned.1.call-update) | async-done | bytes 2097168 | tf_op jit(solution)/shard_map/while/body/eval_jaxpr/psum | solution.py:9
  593.4 8.6 %select_add_fusion.2 = f32[512,2048]{1,0:T(8,128)} fusion(f32[512,2048]{1,0:T(8,128)} %get-tuple-element.215, f32[512,256]{1,0:T(8,128)} %all-reduce.3.cloned.1.call-done, f32[256,2048]{1,0:T(8,128)} %all-reduce.5.cloned.1.call-done, pred[]{:T(512)S(6)} %compare.9), kind=kOutput, calls=%fused_computation.clone.1 | convolution fusion | flops 3223322624 | bytes 11010049 | tf_op jit(solution)/shard_map/while/body/eval_jaxpr/dot_general | solution.py:20
  602.0 0.0 reduce-scatter.2.cloned.1.call-start
  602.0 0.6 reduce-scatter.2.cloned.1.call-update
  602.6 49.1 %reduce-scatter.2.cloned.1.call-done = f32[512,512]{1,0:T(8,128)} async-done(((f32[512,2048]{1,0:T(8,128)}), f32[512,512]{1,0:T(8,128)}) %reduce-scatter.2.cloned.1.call-update) | async-done | bytes 1048592 | tf_op jit(solution)/shard_map/reduce_scatter | solution.py:42
  651.7 2.3 broadcast_multiply_fusion
  (1 shorter events, 0.0 us)
Async XLA Ops:
  6.5 39.6 %all-gather.2.cloned.1.call-start = ((), (), s32[]{:S(2)}) async-start(), calls=%async_computation.1 | async-start | bytes 2621440 | tf_op jit(solution)/shard_map/all_gather | solution.py:39
  46.1 72.9 %all-reduce.3.cloned.1.call-start = ((), (), s32[]{:S(2)}) async-start(), calls=%async_computation.3 | async-start | bytes 1048576 | tf_op jit(solution)/shard_map/while/body/eval_jaxpr/psum | solution.py:9
  47.0 270.8 %all-reduce.5.cloned.1.call-start = ((), (), s32[]{:S(2)}) async-start(), calls=%async_computation.4 | async-start | bytes 4194304 | tf_op jit(solution)/shard_map/while/body/eval_jaxpr/psum | solution.py:9
  325.2 69.7 %all-reduce.3.cloned.1.call-start = ((), (), s32[]{:S(2)}) async-start(), calls=%async_computation.3 | async-start | bytes 1048576 | tf_op jit(solution)/shard_map/while/body/eval_jaxpr/psum | solution.py:9
  326.0 267.4 %all-reduce.5.cloned.1.call-start = ((), (), s32[]{:S(2)}) async-start(), calls=%async_computation.4 | async-start | bytes 4194304 | tf_op jit(solution)/shard_map/while/body/eval_jaxpr/psum | solution.py:9
  602.0 49.7 %reduce-scatter.2.cloned.1.call-start = ((), (), s32[]{:S(2)}) async-start(), calls=%async_computation.2 | async-start | bytes 5242880 | tf_op jit(solution)/shard_map/reduce_scatter | solution.py:42
Sparse Core Ops, SparseCore 0:
  9.1 36.9 all-gather.1
  49.6 69.4 all-reduce.2
  121.7 195.9 all-reduce.4
  328.3 66.5 all-reduce.2
  397.4 195.9 all-reduce.4
  605.0 46.6 reduce-scatter.1
where the time goes:
time: 661 us
  waiting for transfers between devices  610 us (92%)
  matrix products  16 us (2%)
  between operations  13.4 us (2%)
  blocking collectives  12.8 us (2%)
  other arithmetic  8.69 us (1%)
    psum x4, waiting for transfers between devices, from_root(): return lax.psum(block, axis)  533 us
    reduce_scatter x1, waiting for transfers between devices, shards(): lax.psum_scatter(partial_sum, 'layer', scatter_dimension=1, tiled=True)  49.1 us
    all_gather x1, waiting for transfers between devices, shards(): int_panel = lax.all_gather(integrals, 'layer', axis=0, tiled=True)  25.9 us
    dot_general x2, matrix products, one_turn(): jnp.dot(amp_block, int_block, precision=lax.Precision.HIGHEST, preferred_...  16 us
  transfers between devices with their start and end apart: 6, of which 6 were waited for; matrix products, arithmetic and copies ran while one was open for 1% of the time, Pallas kernels for 0%

commit v1 on v0

v1 whole, which is shorter than its diff:
```python
import jax
import jax.numpy as jnp
from jax import lax
from jax.experimental import pallas as pl
from jax.experimental.pallas import tpu as pltpu
from jax.sharding import PartitionSpec as P

MESH = pl.DeviceIdType.MESH
F32, BF16 = jnp.float32, jnp.bfloat16
STEPS = (0, -1, 1, 2)


def split(v):
    hi = v.astype(BF16)
    return hi, (v - hi.astype(F32)).astype(BF16)


def kernel(
    a_ref, b_ref, o_ref, abuf, bbuf, acat, bcat,
    local_sem, a_recv, b_recv, a_send, b_send, y_send, relay_send,
):
    row, col, y = lax.axis_index("row"), lax.axis_index("col"), lax.axis_index("layer")
    x, zh, zl, q = row // 2, row % 2, col // 2, col % 2
    z = zh * 4 + zl

    def device(x_at, y_at, z_at, q_at):
        x_at, y_at, z_at = (x_at + 4) % 4, (y_at + 4) % 4, (z_at + 8) % 8
        return (x_at * 2 + z_at // 4, (z_at % 4) * 2 + q_at, y_at)

    right_x, left_x = device(x + 1, y, z, q), device(x - 1, y, z, q)
    over_z = device(x, y, z + 4, q)
    up_z, down_z = device(x, y, z + 1, q), device(x, y, z - 1, q)
    partner = device(x, y, z, 1 - q)
    y_to = [device(x, y + d, z, q) for d in (1, -1, 2)]

    def at_y(d):
        return (y + d + 4) % 4

    def at_x(d):
        return (x + d + 4) % 4

    def remote(src, dst, send, recv, to):
        return pltpu.make_async_remote_copy(
            src_ref=src, dst_ref=dst, send_sem=send, recv_sem=recv, device_id=to, device_id_type=MESH
        )

    def b_cols(y_at):
        return b_ref.at[:, pl.ds(pl.multiple_of(y_at * 512, 512), 512)]

    sent = []

    def go(copy, cond=None):
        if cond is None:
            copy.start()
        else:
            pl.when(cond)(copy.start)
        sent.append((copy, cond))

    def b_wait(h, y_at, x_at, part=None):
        dst = bbuf.at[h, y_at, x_at] if part is None else bbuf.at[h, y_at, x_at, pl.ds(part * 32, 32)]
        sem = b_recv.at[h, y_at, x_at, 0 if part is None else part]
        pltpu.make_async_copy(dst, dst, sem).wait()

    def b_spread(h, y_at, src, over):
        dst, recv = bbuf.at[h, y_at, x], b_recv.at[h, y_at, x, 0]
        go(remote(src, dst, b_send.at[h, y_at, 0], recv, right_x))
        go(remote(src, dst, b_send.at[h, y_at, 1], recv, left_x))
        if over:
            go(remote(src, dst, b_send.at[h, y_at, 2], recv, over_z))

    def b_own(k, h, over):
        y_at = at_y(STEPS[k])
        b_wait(h, y_at, x)
        b_spread(h, y_at, bbuf.at[h, y_at, x], over)

    def b_relay(k, h):
        y_at = at_y(STEPS[k])
        for part, (d, to) in enumerate(((-1, right_x), (1, left_x))):
            x_at = at_x(d)
            b_wait(h, y_at, x_at)
            half = bbuf.at[h, y_at, x_at, pl.ds(part * 32, 32)]
            go(remote(half, half, relay_send.at[h, y_at, part], b_recv.at[h, y_at, x_at, part], to))

    def a_wait(q_at, y_at, zl_at):
        dst = abuf.at[q_at, y_at, zl_at]
        pltpu.make_async_copy(dst, dst, a_recv.at[q_at, y_at, zl_at]).wait()

    def a_copy(y_at, zl_at, i, to, own=False):
        blk = abuf.at[q, y_at, zl_at]
        return remote(a_ref if own else blk, blk, a_send.at[y_at, zl_at, i], a_recv.at[q, y_at, zl_at], to)

    def both(*conds):
        out = None
        for c in conds:
            if c is not None:
                out = c if out is None else jnp.logical_and(out, c)
        return out

    slots = [(0, None, 0)]
    for s in (1, 2, 3):
        slots += [(-s, zl >= s, 1), (s, zl + s <= 3, -1)]

    def a_slot(i):
        d, cond, way = slots[i]
        zl_at = jnp.clip(zl + d, 0, 3)
        if way != 0:
            pl.when(cond)(lambda: a_wait(q, y, zl_at))
        if way >= 0:
            go(a_copy(y, zl_at, 0, up_z, way == 0), both(cond, zl <= 2))
        if way <= 0:
            go(a_copy(y, zl_at, 1, down_z, way == 0), both(cond, zl >= 1))
        for n in range(3):
            go(a_copy(y, zl_at, 2 + n, y_to[n], way == 0), cond)
        go(a_copy(y, zl_at, 5, partner, way == 0), cond)

    def a_from_y(i):
        d, cond, _ = slots[i]
        zl_at = jnp.clip(zl + d, 0, 3)
        for dy in (-1, 1, 2):
            y_at = at_y(dy)
            if cond is None:
                a_wait(q, y_at, zl_at)
            else:
                pl.when(cond)(lambda: a_wait(q, y_at, zl_at))
            go(a_copy(y_at, zl_at, 5, partner), cond)

    def a_partner(y_at):
        for zl_at in range(4):
            a_wait(1 - q, y_at, zl_at)

    def compute(k, h, first=False):
        y_at = at_y(STEPS[k])
        for i in range(4):
            for rows in range(0, 512, 128):
                if i % 2 == 0:
                    v = jnp.concatenate([abuf[h, y_at, i, :, rows:rows + 128], abuf[h, y_at, i + 1, :, rows:rows + 128]], axis=0)
                    hi, lo = split(v.T)
                    cols = i * 64
                    acat[rows:rows + 128, cols:cols + 128] = hi
                    acat[rows:rows + 128, 256 + cols:256 + cols + 128] = hi
                    acat[rows:rows + 128, 512 + cols:512 + cols + 128] = lo
        for i in range(4):
            hi, lo = split(bbuf[h, y_at, i])
            bcat[i * 64:i * 64 + 64] = hi
            bcat[256 + i * 64:256 + i * 64 + 64] = lo
            bcat[512 + i * 64:512 + i * 64 + 64] = hi

        def tile(t, _):
            rows = pl.ds(pl.multiple_of(t * 256, 256), 256)
            d = jnp.dot(acat[rows, :], bcat[...], preferred_element_type=F32)
            total = d if first else o_ref[rows, :] + d
            o_ref[rows, :] = total
            return 0

        lax.fori_loop(0, 2, tile, 0)

    a_in = pltpu.make_async_copy(a_ref, abuf.at[q, y, zl], local_sem.at[0])
    a_in.start()
    b_in = pltpu.make_async_copy(b_cols(y), bbuf.at[zh, y, x], local_sem.at[1])
    b_in.start()
    barrier = pltpu.get_barrier_semaphore()
    near = [right_x, left_x, over_z, up_z, down_z, partner] + y_to
    for to in near:
        pl.semaphore_signal(barrier, inc=1, device_id=to, device_id_type=MESH)
    pl.semaphore_wait(barrier, len(near))

    b_spread(zh, y, b_cols(y), True)
    for n, d in enumerate((1, -1, 2)):
        go(remote(b_cols(at_y(d)), bbuf.at[zh, y, x], y_send.at[n], b_recv.at[zh, y, x, 0], y_to[n]))
    a_slot(0)
    a_in.wait()
    b_in.wait()

    oh = 1 - zh
    b_own(1, zh, True)
    b_own(2, zh, True)
    a_slot(1)
    a_slot(2)
    b_relay(0, zh)
    b_own(3, zh, True)
    a_slot(3)
    a_slot(4)
    b_relay(1, zh)
    a_slot(5)
    a_slot(6)
    b_relay(2, zh)
    a_from_y(0)
    b_own(0, oh, False)
    a_from_y(1)
    a_from_y(2)
    b_relay(3, zh)
    a_from_y(3)
    a_from_y(4)
    a_from_y(5)
    a_from_y(6)
    b_own(1, oh, False)
    b_relay(0, oh)

    def b_far(k, h):
        b_wait(h, at_y(STEPS[k]), at_x(2), 0)
        b_wait(h, at_y(STEPS[k]), at_x(2), 1)

    for k in range(4):
        a_partner(at_y(STEPS[k]))
    b_far(0, zh)
    compute(0, zh, first=True)
    b_far(1, zh)
    compute(1, zh)
    b_own(2, oh, False)
    b_relay(1, oh)
    b_far(2, zh)
    compute(2, zh)
    b_far(3, zh)
    compute(3, zh)
    b_own(3, oh, False)
    b_relay(2, oh)
    b_far(0, oh)
    compute(0, oh)
    b_far(1, oh)
    compute(1, oh)
    b_relay(3, oh)
    b_far(2, oh)
    compute(2, oh)
    b_far(3, oh)
    compute(3, oh)
    for copy, cond in sent:
        if cond is None:
            copy.wait_send()
        else:
            pl.when(cond)(copy.wait_send)


def shards(amplitudes, integrals):
    dma = pltpu.SemaphoreType.DMA
    product = pl.pallas_call(
        kernel,
        out_shape=jax.ShapeDtypeStruct((512, 512), F32),
        in_specs=[pl.BlockSpec(memory_space=pltpu.MemorySpace.HBM)] * 2,
        out_specs=pl.BlockSpec(memory_space=pltpu.VMEM),
        scratch_shapes=[
            pltpu.VMEM((2, 4, 4, 64, 512), F32),
            pltpu.VMEM((2, 4, 4, 64, 512), F32),
            pltpu.VMEM((512, 768), BF16),
            pltpu.VMEM((768, 512), BF16),
            dma((2,)),
            dma((2, 4, 4)),
            dma((2, 4, 4, 2)),
            dma((4, 4, 6)),
            dma((2, 4, 3)),
            dma((3,)),
            dma((2, 4, 2)),
        ],
        compiler_params=pltpu.CompilerParams(
            collective_id=0, has_side_effects=True, vmem_limit_bytes=24 * 1024 * 1024
        ),
        name="ladder",
    )(amplitudes.T, integrals)
    return 0.5 * product


def solution(mesh):
    in_specs = (P("row", ("col", "layer")), P(("row", "layer"), "col"))
    out_specs = P("row", ("col", "layer"))
    return jax.shard_map(shards, mesh=mesh, in_specs=in_specs, out_specs=out_specs, check_vma=False)
```

time: 661 us -> 73.5 us (0.11)
  waiting for transfers between devices: 610 us -> 0 us
  Pallas kernels: 0 us -> 70.4 us
  matrix products: 16 us -> 0 us
  between operations: 13.4 us -> 0.01 us
  blocking collectives: 12.8 us -> 0 us
  other arithmetic: 8.69 us -> 1.07 us
    psum x4 -> x0, waiting for transfers between devices: 533 us -> none  [from_root(): return lax.psum(block, axis)]
    pallas_call x0 -> x1, Pallas kernels: none -> 70.4 us  [shards(): pl.pallas_call(kernel, out_shape=jax.ShapeDtypeStruct((512, 512), F32), i...]
    reduce_scatter x1 -> x0, waiting for transfers between devices: 49.1 us -> none  [shards(): lax.psum_scatter(partial_sum, 'layer', scatter_dimension=1, tiled=True)]
    all_gather x1 -> x0, waiting for transfers between devices: 25.9 us -> none  [shards(): int_panel = lax.all_gather(integrals, 'layer', axis=0, tiled=True)]
    dot_general x2 -> x0, matrix products: 16 us -> none  [one_turn(): jnp.dot(amp_block, int_block, precision=lax.Precision.HIGHEST, preferred_...]
    all_gather x1 -> x0, blocking collectives: 12.8 us -> none  [shards(): amp_panel = lax.all_gather(amplitudes, 'layer', axis=1, tiled=True)]
  transfers between devices with their start and end apart: 6 -> 0, of which waited for: 6 -> 0; matrix products, arithmetic and copies ran while one was open for 1% -> 0% of each run, Pallas kernels for 0% -> 0%
where the time goes in v1:
time: 73.5 us; the launch traced here: 73.4 us
  Pallas kernels  70.4 us (96%)
  local copies, waits for them, and re-layouts  1.94 us (3%)
  other arithmetic  1.07 us (1%)
    pallas_call x1, Pallas kernels, shards(): pl.pallas_call(kernel, out_shape=jax.ShapeDtypeStruct((512, 512), F32), i...  70.4 us
    unnamed x4, local copies, waits for them, and re-layouts  1.94 us

profile of v1, /device:TPU:1, one launch (start us, length us, event | category | flops | bytes accessed | tf_op | source)
XLA Modules:
  0.0 73.4 jit_solution(3930551484606071568)
XLA Ops:
  0.0 0.0 copy-start
  0.0 1.0 %copy-done = f32[64,2048]{1,0:T(8,128)S(1)} copy-done((f32[64,2048]{1,0:T(8,128)S(1)}, f32[64,2048]{1,0:T(8,128)}, u32[]{:S(2)}) %copy-start) | copy-done | bytes 524312
  1.0 0.0 copy-start.1
  1.0 0.9 %copy-done.1 = f32[512,64]{0,1:T(8,128)S(1)} copy-done((f32[512,64]{0,1:T(8,128)S(1)}, f32[512,64]{0,1:T(8,128)}, u32[]{:S(2)}) %copy-start.1) | copy-done | bytes 131096
  1.9 70.4 %ladder.1 = f32[512,512]{1,0:T(8,128)S(1)} custom-call(f32[64,512]{1,0:T(8,128)S(1)} %bitcast.1, f32[64,2048]{1,0:T(8,128)S(1)} %copy-done), custom_call_target="tpu_custom_call" | custom-call | tf_op jit(solution)/shard_map/ladder/pallas_call | solution.py:235
  72.3 1.1 %broadcast_multiply_fusion = f32[512,512]{1,0:T(8,128)} fusion(f32[512,512]{1,0:T(8,128)S(1)} %ladder.1), kind=kLoop, calls=%fused_computation | loop fusion | flops 262144 | bytes 2097152 | tf_op jit(solution)/shard_map/mul | solution.py:258
Async XLA Ops:
  0.0 1.0 %copy-start = (f32[64,2048]{1,0:T(8,128)S(1)}, f32[64,2048]{1,0:T(8,128)}, u32[]{:S(2)}) copy-start(f32[64,2048]{1,0:T(8,128)} %b_ref.1) | copy-start | bytes 1572868
  1.0 0.9 %copy-start.1 = (f32[512,64]{0,1:T(8,128)S(1)}, f32[512,64]{0,1:T(8,128)}, u32[]{:S(2)}) copy-start(f32[512,64]{0,1:T(8,128)} %param.2) | copy-start | bytes 393220

commit v2 on v1

v2 whole, which is shorter than its diff:
```python
import jax
import jax.numpy as jnp
from jax import lax
from jax.experimental import pallas as pl
from jax.experimental.pallas import tpu as pltpu
from jax.sharding import PartitionSpec as P

MESH = pl.DeviceIdType.MESH
F32, BF16 = jnp.float32, jnp.bfloat16
STEPS = (0, -1, 1, 2)
NEAR, FAR = 1, 2
PIECES = max(NEAR, FAR)


def split(v):
    hi = v.astype(BF16)
    return hi, (v - hi.astype(F32)).astype(BF16)


def kernel(
    a_ref, b_ref, o_ref, abuf, bbuf, acat, bcat,
    local_sem, a_recv, b_recv, a_send, x_send, z_send, y_send, relay_send,
):
    row, col, y = lax.axis_index("row"), lax.axis_index("col"), lax.axis_index("layer")
    x, zh, zl, q = row // 2, row % 2, col // 2, col % 2
    z, oh = zh * 4 + zl, 1 - zh

    def device(x_at, y_at, z_at, q_at):
        x_at, y_at, z_at = (x_at + 4) % 4, (y_at + 4) % 4, (z_at + 8) % 8
        return (x_at * 2 + z_at // 4, (z_at % 4) * 2 + q_at, y_at)

    right_x, left_x = device(x + 1, y, z, q), device(x - 1, y, z, q)
    over_z = device(x, y, z + 4, q)
    up_z, down_z = device(x, y, z + 1, q), device(x, y, z - 1, q)
    partner = device(x, y, z, 1 - q)
    y_to = [device(x, y + d, z, q) for d in (1, -1, 2)]

    def at_y(k):
        return (y + STEPS[k] + 4) % 4

    def at_x(d):
        return (x + d + 4) % 4

    def remote(src, dst, send, recv, to):
        return pltpu.make_async_remote_copy(
            src_ref=src, dst_ref=dst, send_sem=send, recv_sem=recv, device_id=to, device_id_type=MESH
        )

    def wait(dst, sem):
        pltpu.make_async_copy(dst, dst, sem).wait()

    def b_cols(y_at):
        return b_ref.at[:, pl.ds(pl.multiple_of(y_at * 512, 512), 512)]

    sent = []

    def go(copy, cond=None):
        if cond is None:
            copy.start()
        else:
            pl.when(cond)(copy.start)
        sent.append((copy, cond))

    def pieces(h):
        return NEAR if h is zh else FAR

    def b_rows(h, y_at, x_at, p, part=None):
        n = 64 // pieces(h)
        if part is None:
            return bbuf.at[h, y_at, x_at, pl.ds(p * n, n)]
        return bbuf.at[h, y_at, x_at, pl.ds(p * n + part * (n // 2), n // 2)]

    def to_x(k, h, p, src=None):
        y_at = at_y(k)
        dst = b_rows(h, y_at, x, p)
        n = 64 // pieces(h)
        src = dst if src is None else src.at[pl.ds(p * n, n)]
        go(remote(src, dst, x_send.at[h, y_at, p, 0], b_recv.at[h, y_at, x, 2 * p], right_x))
        go(remote(src, dst, x_send.at[h, y_at, p, 1], b_recv.at[h, y_at, x, 2 * p], left_x))

    def to_z(k, p):
        y_at, n = at_y(k), 64 // FAR
        dst = bbuf.at[zh, y_at, x, pl.ds(p * n, n)]
        src = b_cols(y).at[pl.ds(p * n, n)] if k == 0 else dst
        go(remote(src, dst, z_send.at[y_at, p], b_recv.at[zh, y_at, x, 2 * p], over_z))

    def own(k, p):
        wait(b_rows(zh, at_y(k), x, p), b_recv.at[zh, at_y(k), x, 2 * p])
        to_x(k, zh, p)

    def to_y(d, p):
        n = 64 // NEAR
        i = (1, -1, 2).index(d)
        src = b_cols((y + d + 4) % 4).at[pl.ds(p * n, n)]
        go(remote(src, b_rows(zh, y, x, p), y_send.at[i, p], b_recv.at[zh, y, x, 2 * p], y_to[i]))

    def far(k, p):
        wait(b_rows(oh, at_y(k), x, p), b_recv.at[oh, at_y(k), x, 2 * p])
        to_x(k, oh, p)

    def relay(k, h, p=0):
        y_at = at_y(k)
        for part, (d, to) in enumerate(((-1, right_x), (1, left_x))):
            x_at = at_x(d)
            wait(b_rows(h, y_at, x_at, p), b_recv.at[h, y_at, x_at, 2 * p])
            half = b_rows(h, y_at, x_at, p, part)
            go(remote(half, half, relay_send.at[h, y_at, p, part], b_recv.at[h, y_at, x_at, 2 * p + part], to))

    def last(k, h):
        for p in range(pieces(h)):
            for part in range(2):
                wait(b_rows(h, at_y(k), at_x(2), p, part), b_recv.at[h, at_y(k), at_x(2), 2 * p + part])

    def a_wait(q_at, y_at, zl_at):
        wait(abuf.at[q_at, y_at, zl_at], a_recv.at[q_at, y_at, zl_at, 0])

    def a_half(y_at, zl_at, part):
        return abuf.at[q, y_at, zl_at, pl.ds(part * 32, 32)]

    def a_copy(y_at, zl_at, i, to, mine=False):
        blk = abuf.at[q, y_at, zl_at]
        return remote(a_ref if mine else blk, blk, a_send.at[y_at, zl_at, i], a_recv.at[q, y_at, zl_at, 0], to)

    slots = [(0, None, 0)]
    for s in (1, 2, 3):
        slots += [(-s, zl >= s, 1), (s, zl + s <= 3, -1)]

    def both(a, b):
        return b if a is None else jnp.logical_and(a, b)

    def a_along_z(i):
        d, cond, way = slots[i]
        zl_at = jnp.clip(zl + d, 0, 3)
        if way != 0:
            pl.when(cond)(lambda: a_wait(q, y, zl_at))
        if way >= 0:
            go(a_copy(y, zl_at, 0, up_z, way == 0), both(cond, zl <= 2))
        if way <= 0:
            go(a_copy(y, zl_at, 1, down_z, way == 0), both(cond, zl >= 1))

    def a_along_y(i):
        d, cond, way = slots[i]
        zl_at = jnp.clip(zl + d, 0, 3)
        for n in range(2):
            go(a_copy(y, zl_at, 2 + n, y_to[n], way == 0), cond)
        go(a_copy(y, zl_at, 5, partner, way == 0), cond)

    def a_slot(i):
        a_along_z(i)
        a_along_y(i)

    def a_from_y(i):
        d, cond, _ = slots[i]
        zl_at = jnp.clip(zl + d, 0, 3)

        def arrived(y_at):
            a_wait(q, y_at, zl_at)

        for part, k in enumerate((1, 2)):
            y_at = at_y(k)
            if cond is None:
                arrived(y_at)
            else:
                pl.when(cond)(lambda: arrived(y_at))
            half = a_half(y_at, zl_at, part)
            go(remote(half, half, a_send.at[y_at, zl_at, 4], a_recv.at[q, y_at, zl_at, part], y_to[part]), cond)
            go(a_copy(y_at, zl_at, 5, partner), cond)

    def a_far_y(i):
        d, cond, _ = slots[i]
        zl_at = jnp.clip(zl + d, 0, 3)
        y_at = at_y(3)

        def arrived():
            for part in range(2):
                wait(a_half(y_at, zl_at, part), a_recv.at[q, y_at, zl_at, part])

        if cond is None:
            arrived()
        else:
            pl.when(cond)(arrived)
        go(a_copy(y_at, zl_at, 5, partner), cond)

    def a_partner(k):
        for zl_at in range(4):
            a_wait(1 - q, at_y(k), zl_at)

    def a_ready(k, h):
        y_at = at_y(k)
        for p in range(2):
            for rows in range(0, 512, 128):
                v = jnp.concatenate(
                    [abuf[h, y_at, i, p * 32:p * 32 + 32, rows:rows + 128] for i in range(4)], axis=0
                )
                hi, lo = split(v.T)
                acat[p, rows:rows + 128, 0:128] = hi
                acat[p, rows:rows + 128, 128:256] = hi
                acat[p, rows:rows + 128, 256:384] = lo

    def b_ready(k, h, p):
        y_at = at_y(k)
        for i in range(4):
            hi, lo = split(bbuf[h, y_at, i, p * 32:p * 32 + 32, :])
            bcat[p, i * 32:i * 32 + 32] = hi
            bcat[p, 128 + i * 32:128 + i * 32 + 32] = lo
            bcat[p, 256 + i * 32:256 + i * 32 + 32] = hi

    def multiply(groups, first=False):
        def tile(t, _):
            rows = pl.ds(pl.multiple_of(t * 256, 256), 256)
            lhs = jnp.concatenate([acat[p, rows, :] for p in groups], axis=1)
            rhs = jnp.concatenate([bcat[p] for p in groups], axis=0)
            d = jnp.dot(lhs, rhs, preferred_element_type=F32)
            o_ref[rows, :] = d if first else o_ref[rows, :] + d
            return 0

        lax.fori_loop(0, 2, tile, 0)

    def compute(k, h, first=False):
        last(k, h)
        a_ready(k, h)
        b_ready(k, h, 0)
        b_ready(k, h, 1)
        multiply((0, 1), first)

    def last_piece(k, h, p):
        for part in range(2):
            wait(b_rows(h, at_y(k), at_x(2), p, part), b_recv.at[h, at_y(k), at_x(2), 2 * p + part])

    a_in = pltpu.make_async_copy(a_ref, abuf.at[q, y, zl], local_sem.at[0])
    a_in.start()
    b_in = pltpu.make_async_copy(b_cols(y), bbuf.at[zh, y, x], local_sem.at[1])
    b_in.start()
    barrier = pltpu.get_barrier_semaphore()
    near = [over_z, right_x, left_x, up_z, down_z, partner] + y_to
    for to in near:
        pl.semaphore_signal(barrier, inc=1, device_id=to, device_id_type=MESH)
    a_in.wait()
    b_in.wait()
    pl.semaphore_wait(barrier, len(near))

    for p in range(NEAR):
        to_x(0, zh, p, b_cols(y))
    for p in range(NEAR):
        to_y(1, p)
        to_y(-1, p)
    a_along_z(0)
    to_z(0, 0)
    for p in range(NEAR):
        to_y(2, p)
    a_along_y(0)
    to_z(0, 1)
    relay(0, zh, 0)
    own(1, 0)
    to_z(1, 0)
    to_z(1, 1)
    own(2, 0)
    to_z(2, 0)
    to_z(2, 1)
    a_along_z(1)
    a_along_y(1)
    a_along_z(2)
    a_along_y(2)
    own(3, 0)
    to_z(3, 0)
    to_z(3, 1)
    relay(1, zh, 0)
    far(0, 0)
    relay(2, zh, 0)
    far(0, 1)
    a_from_y(0)
    relay(3, zh, 0)
    far(1, 0)
    a_from_y(1)
    relay(0, oh, 0)
    far(1, 1)
    a_from_y(2)
    a_far_y(0)
    relay(0, oh, 1)
    far(2, 0)
    a_far_y(1)
    relay(1, oh, 0)
    far(2, 1)
    relay(1, oh, 1)
    a_far_y(2)
    a_along_z(3)
    a_along_y(3)
    a_along_z(4)
    a_along_y(4)
    relay(2, oh, 0)
    far(3, 0)
    relay(2, oh, 1)
    far(3, 1)
    a_along_z(5)
    a_along_y(5)
    a_along_z(6)
    a_along_y(6)
    relay(3, oh, 0)
    a_from_y(3)
    a_from_y(4)
    a_partner(0)
    compute(0, zh, True)
    compute(0, oh)
    relay(3, oh, 1)
    a_from_y(5)
    a_from_y(6)
    a_partner(1)
    compute(1, zh)
    a_partner(2)
    compute(2, zh)
    compute(1, oh)
    compute(2, oh)
    a_far_y(3)
    a_far_y(4)
    a_far_y(5)
    a_far_y(6)
    a_partner(3)
    compute(3, zh)
    a_ready(3, oh)
    for g in range(2):
        for p in range(g * FAR // 2, (g + 1) * FAR // 2):
            last_piece(3, oh, p)
        b_ready(3, oh, g)
        multiply((g,))

    for copy, cond in sent:
        if cond is None:
            copy.wait_send()
        else:
            pl.when(cond)(copy.wait_send)


def shards(amplitudes, integrals):
    dma = pltpu.SemaphoreType.DMA
    hbm = pltpu.MemorySpace.HBM
    product = pl.pallas_call(
        kernel,
        out_shape=pltpu.VMEM((512, 512), F32),
        in_specs=[pl.BlockSpec(memory_space=hbm)] * 2,
        out_specs=pl.BlockSpec(memory_space=pltpu.VMEM),
        scratch_shapes=[
            pltpu.VMEM((2, 4, 4, 64, 512), F32),
            pltpu.VMEM((2, 4, 4, 64, 512), F32),
            pltpu.VMEM((2, 512, 384), BF16),
            pltpu.VMEM((2, 384, 512), BF16),
            dma((2,)),
            dma((2, 4, 4, 2)),
            dma((2, 4, 4, 2 * PIECES)),
            dma((4, 4, 6)),
            dma((2, 4, PIECES, 2)),
            dma((4, PIECES)),
            dma((3, NEAR)),
            dma((2, 4, PIECES, 2)),
        ],
        compiler_params=pltpu.CompilerParams(
            collective_id=0, has_side_effects=True, vmem_limit_bytes=40 * 1024 * 1024
        ),
        name="ladder",
    )(
        pltpu.with_memory_space_constraint(amplitudes.T, hbm),
        pltpu.with_memory_space_constraint(integrals, hbm),
    )
    return 0.5 * product


def solution(mesh):
    in_specs = (P("row", ("col", "layer")), P(("row", "layer"), "col"))
    out_specs = P("row", ("col", "layer"))
    return jax.shard_map(shards, mesh=mesh, in_specs=in_specs, out_specs=out_specs, check_vma=False)
```

time: 73.5 us -> 60.2 us (0.82)
  Pallas kernels: 70.4 us -> 59 us
  local copies, waits for them, and re-layouts: 1.94 us -> 0 us
    pallas_call x1, Pallas kernels: 70.4 us -> 59 us  [shards(): pl.pallas_call(kernel, out_shape=pltpu.VMEM((512, 512), F32), in_specs=[p...]
    unnamed x4 -> x0, local copies, waits for them, and re-layouts: 1.94 us -> none
where the time goes in v2:
time: 60.2 us; the launch traced here: 60.1 us
  Pallas kernels  59 us (98%)
  other arithmetic  1.07 us (2%)
    pallas_call x1, Pallas kernels, shards(): pl.pallas_call(kernel, out_shape=pltpu.VMEM((512, 512), F32), in_specs=[p...  59 us

profile of v2, /device:TPU:1, one launch (start us, length us, event | category | flops | bytes accessed | tf_op | source)
XLA Modules:
  0.0 60.1 jit_solution(17843079909162525420)
XLA Ops:
  0.0 59.0 %ladder.1 = f32[512,512]{1,0:T(8,128)S(1)} custom-call(f32[64,512]{1,0:T(8,128)} %bitcast.1, f32[64,2048]{1,0:T(8,128)} %b_ref.1), custom_call_target="tpu_custom_call" | custom-call | tf_op jit(solution)/shard_map/ladder/pallas_call | solution.py:336
  59.0 1.1 %broadcast_multiply_fusion = f32[512,512]{1,0:T(8,128)} fusion(f32[512,512]{1,0:T(8,128)S(1)} %ladder.1), kind=kLoop, calls=%fused_computation | loop fusion | flops 262144 | bytes 2097152 | tf_op jit(solution)/shard_map/mul | solution.py:363
